TPU v7x, 256 devices: a whole 4x4x8 slice. The times are simulated.
256 devices in a mesh: prop: 8 (over x, core), dom: 32 (over z, y).
Axes of the slice: x: 4, y: 4, z: 8, core: 2. Of those that a mesh axis runs over, the one named last changes fastest.
Arguments:
- states: float32 [8, 128, 64, 128], P('prop', 'dom'), may hold values from -4 to 4
- accepted: int32 [1], replicated, may hold values from 0 to 7
- noise: float32 [8, 128, 64, 128], P('prop', 'dom'), may hold values from -5 to 5
- source: float32 [128, 64, 128], P('dom'), may hold values from -6 to 6
Outputs:
- pressure: float32 [8, 128, 64, 128], P('prop', 'dom')
All inputs are finite; a program needn't handle non-finite values.
Results may differ from a plain program's by a relative error of at most 0.0003.
Values sent between devices are 32-bit elements; how exact they have to be, the bound alone decides.
A program may use at most 128 MiB of HBM per device.

v0:
```python
import math
import jax
import jax.numpy as jnp
from jax import lax
from jax.sharding import PartitionSpec as P

LEVELS = 4
SWEEPS = 2
COARSE_SWEEPS = 64
OMEGA = 0.7
BETA = 0.4
SHRINK = math.sqrt(1.0 - BETA * BETA)
ZSCALE = 16.0


def padded_2(x, sides, width):
    for axis, dim in sides:
        devices, length = (lax.axis_size(axis), x.shape[dim])
        up = [(i, (i + 1) % devices) for i in range(devices - 1)]
        down = [(j, i) for i, j in up]
        last = lax.slice_in_dim(x, length - width, length, axis=dim)
        initial = lax.slice_in_dim(x, 0, width, axis=dim)
        before = lax.ppermute(last, axis, up)
        after = lax.ppermute(initial, axis, down)
        x = jnp.concatenate([before, x, after], axis=dim)
    return x


def from_root(x, axis, root):
    mine = lax.axis_index(axis) == root
    return lax.psum(jnp.where(mine, x, jnp.zeros_like(x)), axis)


def shift_lower(values, axis):
    axis = values.ndim + axis
    count = values.shape[axis]
    kept = lax.slice_in_dim(values, 0, count - 1, axis=axis)
    return jnp.concatenate(
        [jnp.zeros_like(lax.slice_in_dim(values, 0, 1, axis=axis)), kept], axis=axis
    )


def shift_upper(values, axis):
    axis = values.ndim + axis
    count = values.shape[axis]
    kept = lax.slice_in_dim(values, 1, count, axis=axis)
    return jnp.concatenate(
        [kept, jnp.zeros_like(lax.slice_in_dim(values, 0, 1, axis=axis))], axis=axis
    )


def harmonic(first, second):
    return 2.0 * first * second / (first + second)


def coefficients(perm, padded, scale):
    inner_x = harmonic(perm[..., 1:, :], perm[..., :-1, :])
    west = jnp.concatenate([perm[..., :1, :], inner_x], axis=-2)
    east = jnp.concatenate([inner_x, perm[..., -1:, :]], axis=-2)
    inner_y = harmonic(perm[..., 1:], perm[..., :-1])
    south = jnp.concatenate([perm[..., :1], inner_y], axis=-1)
    north = jnp.concatenate([inner_y, perm[..., -1:]], axis=-1)
    below = harmonic(padded[..., :-2, :, :], perm)
    above = harmonic(padded[..., 2:, :, :], perm)
    zfactor = ZSCALE * scale
    parts = [
        west * scale,
        east * scale,
        south * scale,
        north * scale,
        below * zfactor,
        above * zfactor,
    ]
    diagonal = parts[0] + parts[1] + parts[2] + parts[3] + parts[4] + parts[5]
    return parts + [diagonal, OMEGA / diagonal]


def apply_op(values, padded, coefs):
    result = (
        coefs[6] * values - coefs[0] * shift_lower(values, -2) - coefs[1] * shift_upper(values, -2)
    )
    result = result - coefs[2] * shift_lower(values, -1) - coefs[3] * shift_upper(values, -1)
    return result - coefs[4] * padded[..., :-2, :, :] - coefs[5] * padded[..., 2:, :, :]


def sweep(values, right, coefs, pad_z):
    return values + coefs[7] * (right - apply_op(values, pad_z(values), coefs))


def sum_children(values):
    shape = values.shape
    split = values.reshape(shape[:-3] + (shape[-3] // 2, 2, shape[-2] // 2, 2, shape[-1] // 2, 2))
    return split.sum(axis=(-5, -3, -1))


def prolong(values):
    return jnp.repeat(jnp.repeat(jnp.repeat(values, 2, axis=-3), 2, axis=-2), 2, axis=-1)


def zero_pad(values):
    widths = [(0, 0)] * (values.ndim - 3) + [(1, 1), (0, 0), (0, 0)]
    return jnp.pad(values, widths)


def pressure_rim(values):
    return padded_2(values, (("dom", 1),), 1)


def perm_rim(values):
    return padded_2(values, (("dom", 1),), 1)


def coarse_solve(right, perm, level, pad_z, pad_perm):
    coefs = coefficients(perm, pad_perm(perm), 4.0**level)
    start = coefs[7] * right
    return lax.fori_loop(
        0, COARSE_SWEEPS - 1, lambda step, values: sweep(values, right, coefs, pad_z), start
    )


def level_cycle(right, perm, level, pad_z, pad_perm, deeper):
    coefs = coefficients(perm, pad_perm(perm), 4.0**level)
    values = coefs[7] * right
    values = sweep(values, right, coefs, pad_z)
    residue = right - apply_op(values, pad_z(values), coefs)
    update = deeper(sum_children(residue), sum_children(perm) * 0.125, level + 1)
    values = values + prolong(update)
    for step in range(SWEEPS):
        values = sweep(values, right, coefs, pad_z)
    return values


def local_cycle(right, perm, level):
    if level == LEVELS - 1:
        return coarse_solve(right, perm, level, zero_pad, zero_pad)
    return level_cycle(right, perm, level, zero_pad, zero_pad, local_cycle)


def body(states, accepted, noise, source):
    per_device = states.shape[0]
    chosen = accepted[0]
    owner = chosen // per_device
    picked = lax.dynamic_index_in_dim(states, chosen % per_device, 0, keepdims=False)
    current = from_root(picked, "prop", owner)
    theta = SHRINK * current[None] + BETA * noise
    perm = jnp.exp(theta)
    right = source[None]
    gather_level = 2

    def spread_cycle(right_side, field, level):
        if level == gather_level:
            whole_right, whole_perm = (
                lax.all_gather(right_side, "dom", axis=1, tiled=True),
                lax.all_gather(field, "dom", axis=1, tiled=True),
            )
            result = local_cycle(whole_right, whole_perm, level)
            height = right_side.shape[1]
            return lax.dynamic_slice_in_dim(result, lax.axis_index("dom") * height, height, 1)
        return level_cycle(right_side, field, level, pressure_rim, perm_rim, spread_cycle)

    return spread_cycle(right, perm, 0)


def solution(mesh):
    in_specs = (
        P("prop", "dom", None, None),
        P(),
        P("prop", "dom", None, None),
        P("dom", None, None),
    )
    out_specs = P("prop", "dom", None, None)
    return jax.shard_map(body, mesh=mesh, in_specs=in_specs, out_specs=out_specs, check_vma=False)
```

profile of v0, /device:TPU:120, one launch (start us, length us, event | category | flops | bytes accessed | tf_op | source)
XLA Modules:
  0.0 459.8 jit_solution(12875724920466572557)
XLA Ops:
  11.1 65.1 %all-reduce.61.cloned.1.call-done = f32[4,64,128]{1,2,0:T(8,128)} async-done(((f32[4,64,128]{1,2,0:T(8,128)}), f32[4,64,128]{1,2,0:T(8,128)}) %all-reduce.61.cloned.1.call-update) | async-done | bytes 131088 | tf_op jit(solution)/shard_map/psum | solution.py:31
  78.3 9.8 %reshape.767 = f32[2,2,32,2,64,2]{5,4,3,2,1,0:T(8,128)} reshape(f32[1,4,64,128]{3,2,1,0:T(8,128)S(1)} %copy.50) | data formatting | bytes 262144 | tf_op jit(solution)/shard_map/reshape | solution.py:92
  88.1 4.0 reduce_sum.74
  94.8 48.6 %all-gather = f32[512,32]{1,0:T(8,128)S(1)} all-gather(f32[16,32]{1,0:T(8,128)S(1)} %broadcast_multiply_fusion), channel_id=2, replica_groups=mesh['prop'=8,'dom'=32] {'dom'}, dimensions={0}, use_global_device_ids=true | all-gather | bytes 67584 | tf_op jit(solution)/shard_map/all_gather | solution.py:154
  145.8 5.5 %reshape.769 = f32[16,2,8,2,16,2]{3,2,1,0,5,4:T(8,128)} reshape(f32[512,32]{0,1:T(8,128)S(1)} %copy.52) | data formatting | bytes 131072 | tf_op jit(solution)/shard_map/reshape | solution.py:92
  154.2 4.6 collective-permute-start
  160.8 7.2 %collective-permute-start.4 = (f32[1,1,32,64]{3,2,1,0:T(8,128)}, f32[1,1,32,64]{3,2,1,0:T(8,128)S(1)}, u32[]{:S(2)}, u32[]{:S(2)}) collective-permute-start(f32[1,1,32,64]{3,2,1,0:T(8,128)} %get-tuple-element.298), channel_id=1, source_target_pairs={{0,1},{1,2},{2,3},{3,4},{4,5},{5,6},{6,7},{7,8},{8,9},{9,10},{10,1... | collective-permute-start | bytes 24584 | tf_op jit(solution)/shard_map/ppermute | solution.py:23
  179.0 7.2 %collective-permute-start.2 = (f32[1,1,64,128]{2,3,1,0:T(8,128)S(1)}, f32[1,1,64,128]{2,3,1,0:T(8,128)S(1)}, u32[]{:S(2)}, u32[]{:S(2)}) collective-permute-start(f32[1,1,64,128]{2,3,1,0:T(8,128)S(1)} %get-tuple-element.255), channel_id=1, source_target_pairs={{0,1},{1,2},{2,3},{3,4},{4,5},{5,6},{6,7},{7,8},{8,9},{9,10},{10,1... | collective-permute-start | bytes 98312 | tf_op jit(solution)/shard_map/ppermute | solution.py:23
  188.2 7.5 %collective-permute-done.3 = f32[1,1,64,128]{2,3,1,0:T(8,128)S(1)} collective-permute-done((f32[1,1,64,128]{2,3,1,0:T(8,128)S(1)}, f32[1,1,64,128]{2,3,1,0:T(8,128)S(1)}, u32[]{:S(2)}, u32[]{:S(2)}) %collective-permute-start.3) | collective-permute-done | bytes 32800 | tf_op jit(solution)/shard_map/ppermute | solution.py:24
  198.2 3.9 collective-permute-start.7
  202.4 5.2 %collective-permute-done.7 = f32[1,1,64,128]{2,3,1,0:T(8,128)S(1)} collective-permute-done((f32[1,1,64,128]{2,3,1,0:T(8,128)S(1)}, f32[1,1,64,128]{2,3,1,0:T(8,128)S(1)}, u32[]{:S(2)}, u32[]{:S(2)}) %collective-permute-start.7) | collective-permute-done | bytes 32800 | tf_op jit(solution)/shard_map/ppermute | solution.py:24
  208.2 9.8 %reshape.768 = f32[2,2,32,2,64,2]{5,4,3,2,1,0:T(8,128)} reshape(f32[1,4,64,128]{3,2,1,0:T(8,128)S(1)} %copy.51) | data formatting | bytes 262144 | tf_op jit(solution)/shard_map/reshape | solution.py:92
  218.0 4.0 reduce_sum.75
  228.2 4.9 %collective-permute-done.9 = f32[1,1,32,64]{3,2,1,0:T(8,128)S(1)} collective-permute-done((f32[1,1,32,64]{3,2,1,0:T(8,128)S(1)}, f32[1,1,32,64]{3,2,1,0:T(8,128)S(1)}, u32[]{:S(2)}, u32[]{:S(2)}) %collective-permute-start.9) | collective-permute-done | bytes 8224 | tf_op jit(solution)/shard_map/ppermute | solution.py:24
  239.2 4.9 %collective-permute-done.11 = f32[1,1,32,64]{3,2,1,0:T(8,128)S(1)} collective-permute-done((f32[1,1,32,64]{3,2,1,0:T(8,128)S(1)}, f32[1,1,32,64]{3,2,1,0:T(8,128)S(1)}, u32[]{:S(2)}, u32[]{:S(2)}) %collective-permute-start.11) | collective-permute-done | bytes 8224 | tf_op jit(solution)/shard_map/ppermute | solution.py:24
  245.0 46.0 %all-gather.1 = f32[512,32]{1,0:T(8,128)S(1)} all-gather(f32[16,32]{1,0:T(8,128)S(1)} %reduce_sum.82), channel_id=3, replica_groups=mesh['prop'=8,'dom'=32] {'dom'}, dimensions={0}, use_global_device_ids=true | all-gather | bytes 67584 | tf_op jit(solution)/shard_map/all_gather | solution.py:153
  295.8 4.5 reshape.770
  307.9 84.0 %while.15 = (s32[]{:T(128)}, f32[1,16,8,16]{3,2,1,0:T(8,128)S(1)}, f32[1,16,8,16]{3,2,1,0:T(8,128)}, f32[1,16,8,16]{3,2,1,0:T(8,128)}, f32[1,16,8,16]{3,2,1,0:T(...) while((s32[]{:T(128)}, f32[1,16,8,16]{3,2,1,0:T(8,128)S(1)}, ...), condition=%wide.region_10.11_spmd, body=%wide.region_9.10_spmd.sunk | while | flops 32770 | bytes 195701 | solution.py:116
  400.2 4.6 collective-permute-start.12
  406.8 7.0 %collective-permute-done.13 = f32[1,1,32,64]{3,2,1,0:T(8,128)S(1)} collective-permute-done((f32[1,1,32,64]{3,2,1,0:T(8,128)S(1)}, f32[1,1,32,64]{3,2,1,0:T(8,128)S(1)}, u32[]{:S(2)}, u32[]{:S(2)}) %collective-permute-start.13) | collective-permute-done | bytes 8224 | tf_op jit(solution)/shard_map/ppermute | solution.py:24
  420.7 4.9 %collective-permute-done.15 = f32[1,1,32,64]{3,2,1,0:T(8,128)S(1)} collective-permute-done((f32[1,1,32,64]{3,2,1,0:T(8,128)S(1)}, f32[1,1,32,64]{3,2,1,0:T(8,128)S(1)}, u32[]{:S(2)}, u32[]{:S(2)}) %collective-permute-start.15) | collective-permute-done | bytes 8224 | tf_op jit(solution)/shard_map/ppermute | solution.py:24
  428.8 3.9 collective-permute-start.17
  433.1 5.2 %collective-permute-done.17 = f32[1,1,64,128]{2,3,1,0:T(8,128)S(1)} collective-permute-done((f32[1,1,64,128]{2,3,1,0:T(8,128)S(1)}, f32[1,1,64,128]{2,3,1,0:T(8,128)S(1)}, u32[]{:S(2)}, u32[]{:S(2)}) %collective-permute-start.17) | collective-permute-done | bytes 32800 | tf_op jit(solution)/shard_map/ppermute | solution.py:24
  445.8 5.2 %collective-permute-done.19 = f32[1,1,64,128]{2,3,1,0:T(8,128)S(1)} collective-permute-done((f32[1,1,64,128]{2,3,1,0:T(8,128)S(1)}, f32[1,1,64,128]{2,3,1,0:T(8,128)S(1)}, u32[]{:S(2)}, u32[]{:S(2)}) %collective-permute-start.19) | collective-permute-done | bytes 32800 | tf_op jit(solution)/shard_map/ppermute | solution.py:24
  (437 shorter events, 168.9 us)
Async XLA Ops:
  6.5 69.6 %all-reduce.61.cloned.1.call-start = ((), (), s32[]{:S(2)}) async-start(), calls=%async_computation | async-start | bytes 524288 | tf_op jit(solution)/shard_map/psum | solution.py:31
  77.8 129.9 %copy-start.18 = (f32[1,4,64,1]{2,3,1,0:T(1,128)}, f32[1,4,64,1]{2,3,1,0:T(1,128)S(1)}, u32[]{:S(2)}) copy-start(f32[1,4,64,1]{2,3,1,0:T(1,128)S(1)} %get-tuple-element.261) | copy-start | bytes 3076
  77.8 129.9 %copy-start.19 = (f32[1,4,64,1]{2,3,1,0:T(1,128)}, f32[1,4,64,1]{2,3,1,0:T(1,128)S(1)}, u32[]{:S(2)}) copy-start(f32[1,4,64,1]{2,3,1,0:T(1,128)S(1)} %get-tuple-element.262) | copy-start | bytes 3076
  93.3 150.8 %copy-start.8 = (f32[1,2,31,64]{3,2,1,0:T(8,128)}, f32[1,2,31,64]{3,2,1,0:T(8,128)S(1)}, u32[]{:S(2)}) copy-start(f32[1,2,31,64]{3,2,1,0:T(8,128)S(1)} %add_divide_fusion.7) | copy-start | bytes 47620
  154.2 24.2 %collective-permute-start = (f32[1,1,64,128]{2,3,1,0:T(8,128)}, f32[1,1,64,128]{2,3,1,0:T(8,128)S(1)}, u32[]{:S(2)}, u32[]{:S(2)}) collective-permute-start(f32[1,1,64,128]{2,3,1,0:T(8,128)} %get-tuple-element.260), channel_id=1, source_target_pairs={{0,1},{1,2},{2,3},{3,4},{4,5},{5,6},{6,7},{7,8},{8,9},{9,10},{10,1... | collective-permute-start | bytes 98312 | tf_op jit(solution)/shard_map/ppermute | solution.py:23
  158.8 19.6 %collective-permute-start.1 = (f32[1,1,64,128]{2,3,1,0:T(8,128)}, f32[1,1,64,128]{2,3,1,0:T(8,128)S(1)}, u32[]{:S(2)}, u32[]{:S(2)}) collective-permute-start(f32[1,1,64,128]{2,3,1,0:T(8,128)} %get-tuple-element.259), channel_id=1, source_target_pairs={{1,0},{2,1},{3,2},{4,3},{5,4},{6,5},{7,6},{8,7},{9,8},{10,9},{11,1... | collective-permute-start | bytes 98312 | tf_op jit(solution)/shard_map/ppermute | solution.py:24
  160.8 61.3 %collective-permute-start.4 = (f32[1,1,32,64]{3,2,1,0:T(8,128)}, f32[1,1,32,64]{3,2,1,0:T(8,128)S(1)}, u32[]{:S(2)}, u32[]{:S(2)}) collective-permute-start(f32[1,1,32,64]{3,2,1,0:T(8,128)} %get-tuple-element.298), channel_id=1, source_target_pairs={{0,1},{1,2},{2,3},{3,4},{4,5},{5,6},{6,7},{7,8},{8,9},{9,10},{10,1... | collective-permute-start | bytes 24584 | tf_op jit(solution)/shard_map/ppermute | solution.py:23
  168.0 54.1 %collective-permute-start.5 = (f32[1,1,32,64]{3,2,1,0:T(8,128)}, f32[1,1,32,64]{3,2,1,0:T(8,128)S(1)}, u32[]{:S(2)}, u32[]{:S(2)}) collective-permute-start(f32[1,1,32,64]{3,2,1,0:T(8,128)} %get-tuple-element.297), channel_id=1, source_target_pairs={{1,0},{2,1},{3,2},{4,3},{5,4},{6,5},{7,6},{8,7},{9,8},{10,9},{11,1... | collective-permute-start | bytes 24584 | tf_op jit(solution)/shard_map/ppermute | solution.py:24
  179.0 9.2 %collective-permute-start.2 = (f32[1,1,64,128]{2,3,1,0:T(8,128)S(1)}, f32[1,1,64,128]{2,3,1,0:T(8,128)S(1)}, u32[]{:S(2)}, u32[]{:S(2)}) collective-permute-start(f32[1,1,64,128]{2,3,1,0:T(8,128)S(1)} %get-tuple-element.255), channel_id=1, source_target_pairs={{0,1},{1,2},{2,3},{3,4},{4,5},{5,6},{6,7},{7,8},{8,9},{9,10},{10,1... | collective-permute-start | bytes 98312 | tf_op jit(solution)/shard_map/ppermute | solution.py:23
  186.2 9.5 %collective-permute-start.3 = (f32[1,1,64,128]{2,3,1,0:T(8,128)S(1)}, f32[1,1,64,128]{2,3,1,0:T(8,128)S(1)}, u32[]{:S(2)}, u32[]{:S(2)}) collective-permute-start(f32[1,1,64,128]{2,3,1,0:T(8,128)S(1)} %get-tuple-element.256), channel_id=1, source_target_pairs={{1,0},{2,1},{3,2},{4,3},{5,4},{6,5},{7,6},{8,7},{9,8},{10,9},{11,1... | collective-permute-start | bytes 98312 | tf_op jit(solution)/shard_map/ppermute | solution.py:24
  196.3 6.2 %collective-permute-start.6 = (f32[1,1,64,128]{2,3,1,0:T(8,128)S(1)}, f32[1,1,64,128]{2,3,1,0:T(8,128)S(1)}, u32[]{:S(2)}, u32[]{:S(2)}) collective-permute-start(f32[1,1,64,128]{2,3,1,0:T(8,128)S(1)} %get-tuple-element.249), channel_id=1, source_target_pairs={{0,1},{1,2},{2,3},{3,4},{4,5},{5,6},{6,7},{7,8},{8,9},{9,10},{10,1... | collective-permute-start | bytes 98312 | tf_op jit(solution)/shard_map/ppermute | solution.py:23
  198.2 9.5 %collective-permute-start.7 = (f32[1,1,64,128]{2,3,1,0:T(8,128)S(1)}, f32[1,1,64,128]{2,3,1,0:T(8,128)S(1)}, u32[]{:S(2)}, u32[]{:S(2)}) collective-permute-start(f32[1,1,64,128]{2,3,1,0:T(8,128)S(1)} %get-tuple-element.250), channel_id=1, source_target_pairs={{1,0},{2,1},{3,2},{4,3},{5,4},{6,5},{7,6},{8,7},{9,8},{10,9},{11,1... | collective-permute-start | bytes 98312 | tf_op jit(solution)/shard_map/ppermute | solution.py:24
  222.3 5.9 %collective-permute-start.8 = (f32[1,1,32,64]{3,2,1,0:T(8,128)S(1)}, f32[1,1,32,64]{3,2,1,0:T(8,128)S(1)}, u32[]{:S(2)}, u32[]{:S(2)}) collective-permute-start(f32[1,1,32,64]{3,2,1,0:T(8,128)S(1)} %get-tuple-element.293), channel_id=1, source_target_pairs={{0,1},{1,2},{2,3},{3,4},{4,5},{5,6},{6,7},{7,8},{8,9},{9,10},{10,1... | collective-permute-start | bytes 24584 | tf_op jit(solution)/shard_map/ppermute | solution.py:23
  224.2 9.0 %collective-permute-start.9 = (f32[1,1,32,64]{3,2,1,0:T(8,128)S(1)}, f32[1,1,32,64]{3,2,1,0:T(8,128)S(1)}, u32[]{:S(2)}, u32[]{:S(2)}) collective-permute-start(f32[1,1,32,64]{3,2,1,0:T(8,128)S(1)} %get-tuple-element.294), channel_id=1, source_target_pairs={{1,0},{2,1},{3,2},{4,3},{5,4},{6,5},{7,6},{8,7},{9,8},{10,9},{11,1... | collective-permute-start | bytes 24584 | tf_op jit(solution)/shard_map/ppermute | solution.py:24
  233.3 5.9 %collective-permute-start.10 = (f32[1,1,32,64]{3,2,1,0:T(8,128)S(1)}, f32[1,1,32,64]{3,2,1,0:T(8,128)S(1)}, u32[]{:S(2)}, u32[]{:S(2)}) collective-permute-start(f32[1,1,32,64]{3,2,1,0:T(8,128)S(1)} %get-tuple-element.287), channel_id=1, source_target_pairs={{0,1},{1,2},{2,3},{3,4},{4,5},{5,6},{6,7},{7,8},{8,9},{9,10},{10,1... | collective-permute-start | bytes 24584 | tf_op jit(solution)/shard_map/ppermute | solution.py:23
  235.2 9.0 %collective-permute-start.11 = (f32[1,1,32,64]{3,2,1,0:T(8,128)S(1)}, f32[1,1,32,64]{3,2,1,0:T(8,128)S(1)}, u32[]{:S(2)}, u32[]{:S(2)}) collective-permute-start(f32[1,1,32,64]{3,2,1,0:T(8,128)S(1)} %get-tuple-element.288), channel_id=1, source_target_pairs={{1,0},{2,1},{3,2},{4,3},{5,4},{6,5},{7,6},{8,7},{9,8},{10,9},{11,1... | collective-permute-start | bytes 24584 | tf_op jit(solution)/shard_map/ppermute | solution.py:24
  400.2 6.6 %collective-permute-start.12 = (f32[1,1,32,64]{3,2,1,0:T(8,128)S(1)}, f32[1,1,32,64]{3,2,1,0:T(8,128)S(1)}, u32[]{:S(2)}, u32[]{:S(2)}) collective-permute-start(f32[1,1,32,64]{3,2,1,0:T(8,128)S(1)} %get-tuple-element.279), channel_id=1, source_target_pairs={{0,1},{1,2},{2,3},{3,4},{4,5},{5,6},{6,7},{7,8},{8,9},{9,10},{10,1... | collective-permute-start | bytes 24584 | tf_op jit(solution)/shard_map/ppermute | solution.py:23
  404.8 9.0 %collective-permute-start.13 = (f32[1,1,32,64]{3,2,1,0:T(8,128)S(1)}, f32[1,1,32,64]{3,2,1,0:T(8,128)S(1)}, u32[]{:S(2)}, u32[]{:S(2)}) collective-permute-start(f32[1,1,32,64]{3,2,1,0:T(8,128)S(1)} %get-tuple-element.280), channel_id=1, source_target_pairs={{1,0},{2,1},{3,2},{4,3},{5,4},{6,5},{7,6},{8,7},{9,8},{10,9},{11,1... | collective-permute-start | bytes 24584 | tf_op jit(solution)/shard_map/ppermute | solution.py:24
  414.7 5.9 %collective-permute-start.14 = (f32[1,1,32,64]{3,2,1,0:T(8,128)S(1)}, f32[1,1,32,64]{3,2,1,0:T(8,128)S(1)}, u32[]{:S(2)}, u32[]{:S(2)}) collective-permute-start(f32[1,1,32,64]{3,2,1,0:T(8,128)S(1)} %get-tuple-element.273), channel_id=1, source_target_pairs={{0,1},{1,2},{2,3},{3,4},{4,5},{5,6},{6,7},{7,8},{8,9},{9,10},{10,1... | collective-permute-start | bytes 24584 | tf_op jit(solution)/shard_map/ppermute | solution.py:23
  416.7 9.0 %collective-permute-start.15 = (f32[1,1,32,64]{3,2,1,0:T(8,128)S(1)}, f32[1,1,32,64]{3,2,1,0:T(8,128)S(1)}, u32[]{:S(2)}, u32[]{:S(2)}) collective-permute-start(f32[1,1,32,64]{3,2,1,0:T(8,128)S(1)} %get-tuple-element.274), channel_id=1, source_target_pairs={{1,0},{2,1},{3,2},{4,3},{5,4},{6,5},{7,6},{8,7},{9,8},{10,9},{11,1... | collective-permute-start | bytes 24584 | tf_op jit(solution)/shard_map/ppermute | solution.py:24
  426.9 6.2 %collective-permute-start.16 = (f32[1,1,64,128]{2,3,1,0:T(8,128)S(1)}, f32[1,1,64,128]{2,3,1,0:T(8,128)S(1)}, u32[]{:S(2)}, u32[]{:S(2)}) collective-permute-start(f32[1,1,64,128]{2,3,1,0:T(8,128)S(1)} %get-tuple-element.219), channel_id=1, source_target_pairs={{0,1},{1,2},{2,3},{3,4},{4,5},{5,6},{6,7},{7,8},{8,9},{9,10},{10,1... | collective-permute-start | bytes 98312 | tf_op jit(solution)/shard_map/ppermute | solution.py:23
  428.8 9.5 %collective-permute-start.17 = (f32[1,1,64,128]{2,3,1,0:T(8,128)S(1)}, f32[1,1,64,128]{2,3,1,0:T(8,128)S(1)}, u32[]{:S(2)}, u32[]{:S(2)}) collective-permute-start(f32[1,1,64,128]{2,3,1,0:T(8,128)S(1)} %get-tuple-element.220), channel_id=1, source_target_pairs={{1,0},{2,1},{3,2},{4,3},{5,4},{6,5},{7,6},{8,7},{9,8},{10,9},{11,1... | collective-permute-start | bytes 98312 | tf_op jit(solution)/shard_map/ppermute | solution.py:24
  439.6 6.2 %collective-permute-start.18 = (f32[1,1,64,128]{2,3,1,0:T(8,128)S(1)}, f32[1,1,64,128]{2,3,1,0:T(8,128)S(1)}, u32[]{:S(2)}, u32[]{:S(2)}) collective-permute-start(f32[1,1,64,128]{2,3,1,0:T(8,128)S(1)} %get-tuple-element.213), channel_id=1, source_target_pairs={{0,1},{1,2},{2,3},{3,4},{4,5},{5,6},{6,7},{7,8},{8,9},{9,10},{10,1... | collective-permute-start | bytes 98312 | tf_op jit(solution)/shard_map/ppermute | solution.py:23
  441.5 9.5 %collective-permute-start.19 = (f32[1,1,64,128]{2,3,1,0:T(8,128)S(1)}, f32[1,1,64,128]{2,3,1,0:T(8,128)S(1)}, u32[]{:S(2)}, u32[]{:S(2)}) collective-permute-start(f32[1,1,64,128]{2,3,1,0:T(8,128)S(1)} %get-tuple-element.214), channel_id=1, source_target_pairs={{1,0},{2,1},{3,2},{4,3},{5,4},{6,5},{7,6},{8,7},{9,8},{10,9},{11,1... | collective-permute-start | bytes 98312 | tf_op jit(solution)/shard_map/ppermute | solution.py:24
  (19 other events, 460.2 us)
Sparse Core Ops, SparseCore 0:
  9.7 66.4 all-reduce.60
where the time goes:
time: 465 us; the launch traced here: 460 us
  waiting for transfers between devices  111 us (24%)
  other arithmetic  108 us (23%)
  blocking collectives  94.6 us (20%)
  starting transfers between devices  66.4 us (14%)
  local copies, waits for them, and re-layouts  62.8 us (14%)
  between operations  15 us (3%)
    add x71, other arithmetic, sweep(): return values + coefs[7] * (right - apply_op(values, pad_z(values), coefs))  82.6 us
    psum x1, waiting for transfers between devices, from_root(): return lax.psum(jnp.where(mine, x, jnp.zeros_like(x)), axis)  65.1 us
    all_gather x1, blocking collectives, spread_cycle(): lax.all_gather(field, 'dom', axis=1, tiled=True)  48.6 us
    all_gather x1, blocking collectives, spread_cycle(): lax.all_gather(right_side, 'dom', axis=1, tiled=True)  46 us
    ppermute x10, waiting for transfers between devices, padded_2(): after = lax.ppermute(initial, axis, down)  45.1 us
    ppermute x10, starting transfers between devices, padded_2(): before = lax.ppermute(last, axis, up)  35.2 us
    ppermute x10, starting transfers between devices, padded_2(): after = lax.ppermute(initial, axis, down)  31.2 us
    reshape x4, local copies, waits for them, and re-layouts, sum_children(): values.reshape(shape[:-3] + (shape[-3] // 2, 2, shape[-2] // 2, 2, shape[...  29.6 us
  transfers between devices with their start and end apart: 21, of which 12 were waited for; matrix products, arithmetic and copies ran while one was open for 6% of the time, Pallas kernels for 0%

commit v1 on v0

--- a/solution.py
+++ b/solution.py
@@ -28,7 +28,7 @@
 
 def from_root(x, axis, root):
     mine = lax.axis_index(axis) == root
-    return lax.psum(jnp.where(mine, x, jnp.zeros_like(x)), axis)
+    return jnp.sum(lax.all_gather(jnp.where(mine, x, jnp.zeros_like(x)), axis), axis=0)
 
 
 def shift_lower(values, axis):

time: 465 us -> 390 us (0.84)
  waiting for transfers between devices: 111 us -> 73.1 us
  other arithmetic: 108 us -> 86.9 us
  local copies, waits for them, and re-layouts: 62.8 us -> 47.3 us
    psum x1 -> x0, waiting for transfers between devices: 65.1 us -> none  [from_root(): return lax.psum(jnp.where(mine, x, jnp.zeros_like(x)), axis)]
    all_gather x0 -> x1, waiting for transfers between devices: none -> 28.9 us  [from_root(): lax.all_gather(jnp.where(mine, x, jnp.zeros_like(x)), axis)]
    add x71, other arithmetic: 82.6 us -> 63.1 us  [sweep(): return values + coefs[7] * (right - apply_op(values, pad_z(values), coefs))]
    while x10, local copies, waits for them, and re-layouts: 10.3 us -> 3.56 us  [coarse_solve(): lax.fori_loop(0, COARSE_SWEEPS - 1, lambda step, values: sweep(values, ri...]
  transfers between devices with their start and end apart: 21 -> 21, of which waited for: 12 -> 9; matrix products, arithmetic and copies ran while one was open for 6% -> 4% of each run, Pallas kernels for 0% -> 0%
where the time goes in v1:
time: 390 us; the launch traced here: 386 us
  blocking collectives  94.7 us (24%)
  other arithmetic  86.9 us (22%)
  waiting for transfers between devices  73.1 us (19%)
  starting transfers between devices  66.4 us (17%)
  local copies, waits for them, and re-layouts  47.3 us (12%)
  between operations  15.2 us (4%)
    add x71, other arithmetic, sweep(): return values + coefs[7] * (right - apply_op(values, pad_z(values), coefs))  63.1 us
    all_gather x1, blocking collectives, spread_cycle(): lax.all_gather(field, 'dom', axis=1, tiled=True)  48.7 us
    all_gather x1, blocking collectives, spread_cycle(): lax.all_gather(right_side, 'dom', axis=1, tiled=True)  46 us
    ppermute x10, waiting for transfers between devices, padded_2(): after = lax.ppermute(initial, axis, down)  44.2 us
    ppermute x10, starting transfers between devices, padded_2(): before = lax.ppermute(last, axis, up)  35.2 us
    ppermute x10, starting transfers between devices, padded_2(): after = lax.ppermute(initial, axis, down)  31.2 us
    reshape x4, local copies, waits for them, and re-layouts, sum_children(): values.reshape(shape[:-3] + (shape[-3] // 2, 2, shape[-2] // 2, 2, shape[...  29.6 us
    all_gather x1, waiting for transfers between devices, from_root(): lax.all_gather(jnp.where(mine, x, jnp.zeros_like(x)), axis)  28.9 us
  transfers between devices with their start and end apart: 21, of which 9 were waited for; matrix products, arithmetic and copies ran while one was open for 4% of the time, Pallas kernels for 0%

profile of v1, /device:TPU:120, one launch (start us, length us, event | category | flops | bytes accessed | tf_op | source)
XLA Modules:
  0.0 385.6 jit_solution(14852028093009958316)
XLA Ops:
  7.9 28.9 %all-gather.4.cloned.1.call-done = f32[8,4,64,128]{3,2,1,0:T(8,128)} async-done(((f32[1,4,64,128]{3,2,1,0:T(8,128)}), f32[8,4,64,128]{3,2,1,0:T(8,128)}) %all-gather.4.cloned.1.call-update) | async-done | bytes 1048592 | tf_op jit(solution)/shard_map/all_gather | solution.py:31
  39.3 9.8 %reshape.773 = f32[2,2,32,2,64,2]{5,4,3,2,1,0:T(8,128)} reshape(f32[1,4,64,128]{3,2,1,0:T(8,128)S(1)} %fusion.63) | data formatting | bytes 262144 | tf_op jit(solution)/shard_map/reshape | solution.py:92
  49.1 4.0 %reduce_sum.84 = f32[2,32,64]{2,1,0:T(8,128)S(1)} reduce(f32[2,2,32,2,64,2]{5,4,3,2,1,0:T(8,128)} %reshape.773, f32[]{:T(128)} %constant.37.clone.1), dimensions={1,3,5}, to_apply=%region_1.2 | reduce | flops 28672 | bytes 147460 | tf_op jit(solution)/shard_map/reduce_sum | solution.py:93
  54.1 48.7 %all-gather = f32[512,32]{1,0:T(8,128)S(1)} all-gather(f32[16,32]{1,0:T(8,128)S(1)} %broadcast_multiply_fusion), channel_id=2, replica_groups=mesh['prop'=8,'dom'=32] {'dom'}, dimensions={0}, use_global_device_ids=true | all-gather | bytes 67584 | tf_op jit(solution)/shard_map/all_gather | solution.py:154
  105.4 5.5 %reshape.775 = f32[16,2,8,2,16,2]{3,2,1,0,5,4:T(8,128)} reshape(f32[512,32]{0,1:T(8,128)S(1)} %copy.40) | data formatting | bytes 131072 | tf_op jit(solution)/shard_map/reshape | solution.py:92
  113.7 4.6 %collective-permute-start = (f32[1,1,64,128]{3,2,1,0:T(8,128)S(1)}, f32[1,1,64,128]{3,2,1,0:T(8,128)S(1)}, u32[]{:S(2)}, u32[]{:S(2)}) collective-permute-start(f32[1,1,64,128]{3,2,1,0:T(8,128)S(1)} %get-tuple-element.266), channel_id=1, source_target_pairs={{0,1},{1,2},{2,3},{3,4},{4,5},{5,6},{6,7},{7,8},{8,9},{9,10},{10,1... | collective-permute-start | bytes 98312 | tf_op jit(solution)/shard_map/ppermute | solution.py:23
  120.3 7.2 %collective-permute-start.4 = (f32[1,1,32,64]{3,2,1,0:T(8,128)S(1)}, f32[1,1,32,64]{3,2,1,0:T(8,128)S(1)}, u32[]{:S(2)}, u32[]{:S(2)}) collective-permute-start(f32[1,1,32,64]{3,2,1,0:T(8,128)S(1)} %get-tuple-element.298), channel_id=1, source_target_pairs={{0,1},{1,2},{2,3},{3,4},{4,5},{5,6},{6,7},{7,8},{8,9},{9,10},{10,1... | collective-permute-start | bytes 24584 | tf_op jit(solution)/shard_map/ppermute | solution.py:23
  130.8 7.2 %collective-permute-start.2 = (f32[1,1,64,128]{3,2,1,0:T(8,128)S(1)}, f32[1,1,64,128]{3,2,1,0:T(8,128)S(1)}, u32[]{:S(2)}, u32[]{:S(2)}) collective-permute-start(f32[1,1,64,128]{3,2,1,0:T(8,128)S(1)} %get-tuple-element.261), channel_id=1, source_target_pairs={{0,1},{1,2},{2,3},{3,4},{4,5},{5,6},{6,7},{7,8},{8,9},{9,10},{10,1... | collective-permute-start | bytes 98312 | tf_op jit(solution)/shard_map/ppermute | solution.py:23
  140.1 7.1 %collective-permute-done.3 = f32[1,1,64,128]{3,2,1,0:T(8,128)S(1)} collective-permute-done((f32[1,1,64,128]{3,2,1,0:T(8,128)S(1)}, f32[1,1,64,128]{3,2,1,0:T(8,128)S(1)}, u32[]{:S(2)}, u32[]{:S(2)}) %collective-permute-start.3) | collective-permute-done | bytes 32800 | tf_op jit(solution)/shard_map/ppermute | solution.py:24
  149.3 3.9 %collective-permute-start.7 = (f32[1,1,64,128]{3,2,1,0:T(8,128)S(1)}, f32[1,1,64,128]{3,2,1,0:T(8,128)S(1)}, u32[]{:S(2)}, u32[]{:S(2)}) collective-permute-start(f32[1,1,64,128]{3,2,1,0:T(8,128)S(1)} %get-tuple-element.256), channel_id=1, source_target_pairs={{1,0},{2,1},{3,2},{4,3},{5,4},{6,5},{7,6},{8,7},{9,8},{10,9},{11,1... | collective-permute-start | bytes 98312 | tf_op jit(solution)/shard_map/ppermute | solution.py:24
  153.4 5.1 %collective-permute-done.7 = f32[1,1,64,128]{3,2,1,0:T(8,128)S(1)} collective-permute-done((f32[1,1,64,128]{3,2,1,0:T(8,128)S(1)}, f32[1,1,64,128]{3,2,1,0:T(8,128)S(1)}, u32[]{:S(2)}, u32[]{:S(2)}) %collective-permute-start.7) | collective-permute-done | bytes 32800 | tf_op jit(solution)/shard_map/ppermute | solution.py:24
  158.7 9.8 %reshape.774 = f32[2,2,32,2,64,2]{5,4,3,2,1,0:T(8,128)} reshape(f32[1,4,64,128]{3,2,1,0:T(8,128)S(1)} %fusion.43) | data formatting | bytes 262144 | tf_op jit(solution)/shard_map/reshape | solution.py:92
  168.5 4.0 %reduce_sum.85 = f32[2,32,64]{2,1,0:T(8,128)S(1)} reduce(f32[2,2,32,2,64,2]{5,4,3,2,1,0:T(8,128)} %reshape.774, f32[]{:T(128)} %constant.37.clone.1), dimensions={1,3,5}, to_apply=%region_2.3 | reduce | flops 28672 | bytes 147460 | tf_op jit(solution)/shard_map/reduce_sum | solution.py:93
  178.6 4.9 %collective-permute-done.9 = f32[1,1,32,64]{3,2,1,0:T(8,128)S(1)} collective-permute-done((f32[1,1,32,64]{3,2,1,0:T(8,128)S(1)}, f32[1,1,32,64]{3,2,1,0:T(8,128)S(1)}, u32[]{:S(2)}, u32[]{:S(2)}) %collective-permute-start.9) | collective-permute-done | bytes 8224 | tf_op jit(solution)/shard_map/ppermute | solution.py:24
  185.6 3.9 %collective-permute-start.11 = (f32[1,1,32,64]{3,2,1,0:T(8,128)S(1)}, f32[1,1,32,64]{3,2,1,0:T(8,128)S(1)}, u32[]{:S(2)}, u32[]{:S(2)}) collective-permute-start(f32[1,1,32,64]{3,2,1,0:T(8,128)S(1)} %get-tuple-element.288), channel_id=1, source_target_pairs={{1,0},{2,1},{3,2},{4,3},{5,4},{6,5},{7,6},{8,7},{9,8},{10,9},{11,1... | collective-permute-start | bytes 24584 | tf_op jit(solution)/shard_map/ppermute | solution.py:24
  189.6 4.9 %collective-permute-done.11 = f32[1,1,32,64]{3,2,1,0:T(8,128)S(1)} collective-permute-done((f32[1,1,32,64]{3,2,1,0:T(8,128)S(1)}, f32[1,1,32,64]{3,2,1,0:T(8,128)S(1)}, u32[]{:S(2)}, u32[]{:S(2)}) %collective-permute-start.11) | collective-permute-done | bytes 8224 | tf_op jit(solution)/shard_map/ppermute | solution.py:24
  195.4 46.0 %all-gather.1 = f32[512,32]{1,0:T(8,128)S(1)} all-gather(f32[16,32]{1,0:T(8,128)S(1)} %reduce_sum.92), channel_id=3, replica_groups=mesh['prop'=8,'dom'=32] {'dom'}, dimensions={0}, use_global_device_ids=true | all-gather | bytes 67584 | tf_op jit(solution)/shard_map/all_gather | solution.py:153
  246.3 4.5 %reshape.776 = f32[16,2,8,2,16,2]{5,4,3,2,1,0:T(8,128)} reshape(f32[1,32,16,32]{3,2,1,0:T(8,128)} %fusion.17) | data formatting | bytes 131072 | tf_op jit(solution)/shard_map/reshape | solution.py:92
  258.4 67.8 %while.15 = (s32[]{:T(128)}, f32[1,16,8,16]{3,2,1,0:T(8,128)S(1)}, f32[1,16,8,16]{3,2,1,0:T(8,128)S(1)}, f32[1,16,8,16]{3,2,1,0:T(8,128)S(1)}, f32[1,16,8,16]{3,...) while((s32[]{:T(128)}, f32[1,16,8,16]{3,2,1,0:T(8,128)S(1)}, ...), condition=%wide.region_10.11_spmd, body=%wide.region_9.10_spmd.sunk | while | flops 32770 | bytes 195701 | solution.py:116
  330.4 4.6 %collective-permute-start.12 = (f32[1,1,32,64]{3,2,1,0:T(8,128)S(1)}, f32[1,1,32,64]{3,2,1,0:T(8,128)S(1)}, u32[]{:S(2)}, u32[]{:S(2)}) collective-permute-start(f32[1,1,32,64]{3,2,1,0:T(8,128)S(1)} %get-tuple-element.279), channel_id=1, source_target_pairs={{0,1},{1,2},{2,3},{3,4},{4,5},{5,6},{6,7},{7,8},{8,9},{9,10},{10,1... | collective-permute-start | bytes 24584 | tf_op jit(solution)/shard_map/ppermute | solution.py:23
  337.0 7.0 %collective-permute-done.13 = f32[1,1,32,64]{3,2,1,0:T(8,128)S(1)} collective-permute-done((f32[1,1,32,64]{3,2,1,0:T(8,128)S(1)}, f32[1,1,32,64]{3,2,1,0:T(8,128)S(1)}, u32[]{:S(2)}, u32[]{:S(2)}) %collective-permute-start.13) | collective-permute-done | bytes 8224 | tf_op jit(solution)/shard_map/ppermute | solution.py:24
  350.1 4.9 %collective-permute-done.15 = f32[1,1,32,64]{3,2,1,0:T(8,128)S(1)} collective-permute-done((f32[1,1,32,64]{3,2,1,0:T(8,128)S(1)}, f32[1,1,32,64]{3,2,1,0:T(8,128)S(1)}, u32[]{:S(2)}, u32[]{:S(2)}) %collective-permute-start.15) | collective-permute-done | bytes 8224 | tf_op jit(solution)/shard_map/ppermute | solution.py:24
  361.5 5.1 %collective-permute-done.17 = f32[1,1,64,128]{3,2,1,0:T(8,128)S(1)} collective-permute-done((f32[1,1,64,128]{3,2,1,0:T(8,128)S(1)}, f32[1,1,64,128]{3,2,1,0:T(8,128)S(1)}, u32[]{:S(2)}, u32[]{:S(2)}) %collective-permute-start.17) | collective-permute-done | bytes 32800 | tf_op jit(solution)/shard_map/ppermute | solution.py:24
  372.8 5.1 %collective-permute-done.19 = f32[1,1,64,128]{3,2,1,0:T(8,128)S(1)} collective-permute-done((f32[1,1,64,128]{3,2,1,0:T(8,128)S(1)}, f32[1,1,64,128]{3,2,1,0:T(8,128)S(1)}, u32[]{:S(2)}, u32[]{:S(2)}) %collective-permute-start.19) | collective-permute-done | bytes 32800 | tf_op jit(solution)/shard_map/ppermute | solution.py:24
  (443 shorter events, 131.6 us)
Async XLA Ops:
  6.5 30.2 %all-gather.4.cloned.1.call-start = ((), (), s32[]{:S(2)}) async-start(), calls=%async_computation | async-start | bytes 1179648 | tf_op jit(solution)/shard_map/all_gather | solution.py:31
  53.2 141.4 %copy-start.23 = (f32[1,2,1,64]{3,2,1,0:T(1,128)}, f32[1,2,1,64]{3,2,1,0:T(1,128)S(1)}, u32[]{:S(2)}) copy-start(f32[1,2,1,64]{3,2,1,0:T(1,128)S(1)} %get-tuple-element.299) | copy-start | bytes 1540
  53.2 141.4 %copy-start.25 = (f32[1,2,1,64]{3,2,1,0:T(1,128)}, f32[1,2,1,64]{3,2,1,0:T(1,128)S(1)}, u32[]{:S(2)}) copy-start(f32[1,2,1,64]{3,2,1,0:T(1,128)S(1)} %get-tuple-element.300) | copy-start | bytes 1540
  53.2 141.4 %copy-start.4 = (f32[1,2,31,64]{3,2,1,0:T(8,128)}, f32[1,2,31,64]{3,2,1,0:T(8,128)S(1)}, u32[]{:S(2)}) copy-start(f32[1,2,31,64]{3,2,1,0:T(8,128)S(1)} %add_divide_fusion.7) | copy-start | bytes 47620
  113.7 16.8 %collective-permute-start = (f32[1,1,64,128]{3,2,1,0:T(8,128)S(1)}, f32[1,1,64,128]{3,2,1,0:T(8,128)S(1)}, u32[]{:S(2)}, u32[]{:S(2)}) collective-permute-start(f32[1,1,64,128]{3,2,1,0:T(8,128)S(1)} %get-tuple-element.266), channel_id=1, source_target_pairs={{0,1},{1,2},{2,3},{3,4},{4,5},{5,6},{6,7},{7,8},{8,9},{9,10},{10,1... | collective-permute-start | bytes 98312 | tf_op jit(solution)/shard_map/ppermute | solution.py:23
  118.3 12.2 %collective-permute-start.1 = (f32[1,1,64,128]{3,2,1,0:T(8,128)S(1)}, f32[1,1,64,128]{3,2,1,0:T(8,128)S(1)}, u32[]{:S(2)}, u32[]{:S(2)}) collective-permute-start(f32[1,1,64,128]{3,2,1,0:T(8,128)S(1)} %get-tuple-element.265), channel_id=1, source_target_pairs={{1,0},{2,1},{3,2},{4,3},{5,4},{6,5},{7,6},{8,7},{9,8},{10,9},{11,1... | collective-permute-start | bytes 98312 | tf_op jit(solution)/shard_map/ppermute | solution.py:24
  120.3 52.3 %collective-permute-start.4 = (f32[1,1,32,64]{3,2,1,0:T(8,128)S(1)}, f32[1,1,32,64]{3,2,1,0:T(8,128)S(1)}, u32[]{:S(2)}, u32[]{:S(2)}) collective-permute-start(f32[1,1,32,64]{3,2,1,0:T(8,128)S(1)} %get-tuple-element.298), channel_id=1, source_target_pairs={{0,1},{1,2},{2,3},{3,4},{4,5},{5,6},{6,7},{7,8},{8,9},{9,10},{10,1... | collective-permute-start | bytes 24584 | tf_op jit(solution)/shard_map/ppermute | solution.py:23
  127.5 45.0 %collective-permute-start.5 = (f32[1,1,32,64]{3,2,1,0:T(8,128)S(1)}, f32[1,1,32,64]{3,2,1,0:T(8,128)S(1)}, u32[]{:S(2)}, u32[]{:S(2)}) collective-permute-start(f32[1,1,32,64]{3,2,1,0:T(8,128)S(1)} %get-tuple-element.297), channel_id=1, source_target_pairs={{1,0},{2,1},{3,2},{4,3},{5,4},{6,5},{7,6},{8,7},{9,8},{10,9},{11,1... | collective-permute-start | bytes 24584 | tf_op jit(solution)/shard_map/ppermute | solution.py:24
  130.8 9.3 %collective-permute-start.2 = (f32[1,1,64,128]{3,2,1,0:T(8,128)S(1)}, f32[1,1,64,128]{3,2,1,0:T(8,128)S(1)}, u32[]{:S(2)}, u32[]{:S(2)}) collective-permute-start(f32[1,1,64,128]{3,2,1,0:T(8,128)S(1)} %get-tuple-element.261), channel_id=1, source_target_pairs={{0,1},{1,2},{2,3},{3,4},{4,5},{5,6},{6,7},{7,8},{8,9},{9,10},{10,1... | collective-permute-start | bytes 98312 | tf_op jit(solution)/shard_map/ppermute | solution.py:23
  138.0 9.1 %collective-permute-start.3 = (f32[1,1,64,128]{3,2,1,0:T(8,128)S(1)}, f32[1,1,64,128]{3,2,1,0:T(8,128)S(1)}, u32[]{:S(2)}, u32[]{:S(2)}) collective-permute-start(f32[1,1,64,128]{3,2,1,0:T(8,128)S(1)} %get-tuple-element.262), channel_id=1, source_target_pairs={{1,0},{2,1},{3,2},{4,3},{5,4},{6,5},{7,6},{8,7},{9,8},{10,9},{11,1... | collective-permute-start | bytes 98312 | tf_op jit(solution)/shard_map/ppermute | solution.py:24
  147.4 6.0 %collective-permute-start.6 = (f32[1,1,64,128]{3,2,1,0:T(8,128)S(1)}, f32[1,1,64,128]{3,2,1,0:T(8,128)S(1)}, u32[]{:S(2)}, u32[]{:S(2)}) collective-permute-start(f32[1,1,64,128]{3,2,1,0:T(8,128)S(1)} %get-tuple-element.255), channel_id=1, source_target_pairs={{0,1},{1,2},{2,3},{3,4},{4,5},{5,6},{6,7},{7,8},{8,9},{9,10},{10,1... | collective-permute-start | bytes 98312 | tf_op jit(solution)/shard_map/ppermute | solution.py:23
  149.3 9.1 %collective-permute-start.7 = (f32[1,1,64,128]{3,2,1,0:T(8,128)S(1)}, f32[1,1,64,128]{3,2,1,0:T(8,128)S(1)}, u32[]{:S(2)}, u32[]{:S(2)}) collective-permute-start(f32[1,1,64,128]{3,2,1,0:T(8,128)S(1)} %get-tuple-element.256), channel_id=1, source_target_pairs={{1,0},{2,1},{3,2},{4,3},{5,4},{6,5},{7,6},{8,7},{9,8},{10,9},{11,1... | collective-permute-start | bytes 98312 | tf_op jit(solution)/shard_map/ppermute | solution.py:24
  172.7 5.9 %collective-permute-start.8 = (f32[1,1,32,64]{3,2,1,0:T(8,128)S(1)}, f32[1,1,32,64]{3,2,1,0:T(8,128)S(1)}, u32[]{:S(2)}, u32[]{:S(2)}) collective-permute-start(f32[1,1,32,64]{3,2,1,0:T(8,128)S(1)} %get-tuple-element.293), channel_id=1, source_target_pairs={{0,1},{1,2},{2,3},{3,4},{4,5},{5,6},{6,7},{7,8},{8,9},{9,10},{10,1... | collective-permute-start | bytes 24584 | tf_op jit(solution)/shard_map/ppermute | solution.py:23
  174.6 9.0 %collective-permute-start.9 = (f32[1,1,32,64]{3,2,1,0:T(8,128)S(1)}, f32[1,1,32,64]{3,2,1,0:T(8,128)S(1)}, u32[]{:S(2)}, u32[]{:S(2)}) collective-permute-start(f32[1,1,32,64]{3,2,1,0:T(8,128)S(1)} %get-tuple-element.294), channel_id=1, source_target_pairs={{1,0},{2,1},{3,2},{4,3},{5,4},{6,5},{7,6},{8,7},{9,8},{10,9},{11,1... | collective-permute-start | bytes 24584 | tf_op jit(solution)/shard_map/ppermute | solution.py:24
  183.7 5.9 %collective-permute-start.10 = (f32[1,1,32,64]{3,2,1,0:T(8,128)S(1)}, f32[1,1,32,64]{3,2,1,0:T(8,128)S(1)}, u32[]{:S(2)}, u32[]{:S(2)}) collective-permute-start(f32[1,1,32,64]{3,2,1,0:T(8,128)S(1)} %get-tuple-element.287), channel_id=1, source_target_pairs={{0,1},{1,2},{2,3},{3,4},{4,5},{5,6},{6,7},{7,8},{8,9},{9,10},{10,1... | collective-permute-start | bytes 24584 | tf_op jit(solution)/shard_map/ppermute | solution.py:23
  185.6 9.0 %collective-permute-start.11 = (f32[1,1,32,64]{3,2,1,0:T(8,128)S(1)}, f32[1,1,32,64]{3,2,1,0:T(8,128)S(1)}, u32[]{:S(2)}, u32[]{:S(2)}) collective-permute-start(f32[1,1,32,64]{3,2,1,0:T(8,128)S(1)} %get-tuple-element.288), channel_id=1, source_target_pairs={{1,0},{2,1},{3,2},{4,3},{5,4},{6,5},{7,6},{8,7},{9,8},{10,9},{11,1... | collective-permute-start | bytes 24584 | tf_op jit(solution)/shard_map/ppermute | solution.py:24
  330.4 6.6 %collective-permute-start.12 = (f32[1,1,32,64]{3,2,1,0:T(8,128)S(1)}, f32[1,1,32,64]{3,2,1,0:T(8,128)S(1)}, u32[]{:S(2)}, u32[]{:S(2)}) collective-permute-start(f32[1,1,32,64]{3,2,1,0:T(8,128)S(1)} %get-tuple-element.279), channel_id=1, source_target_pairs={{0,1},{1,2},{2,3},{3,4},{4,5},{5,6},{6,7},{7,8},{8,9},{9,10},{10,1... | collective-permute-start | bytes 24584 | tf_op jit(solution)/shard_map/ppermute | solution.py:23
  335.0 9.0 %collective-permute-start.13 = (f32[1,1,32,64]{3,2,1,0:T(8,128)S(1)}, f32[1,1,32,64]{3,2,1,0:T(8,128)S(1)}, u32[]{:S(2)}, u32[]{:S(2)}) collective-permute-start(f32[1,1,32,64]{3,2,1,0:T(8,128)S(1)} %get-tuple-element.280), channel_id=1, source_target_pairs={{1,0},{2,1},{3,2},{4,3},{5,4},{6,5},{7,6},{8,7},{9,8},{10,9},{11,1... | collective-permute-start | bytes 24584 | tf_op jit(solution)/shard_map/ppermute | solution.py:24
  344.1 5.9 %collective-permute-start.14 = (f32[1,1,32,64]{3,2,1,0:T(8,128)S(1)}, f32[1,1,32,64]{3,2,1,0:T(8,128)S(1)}, u32[]{:S(2)}, u32[]{:S(2)}) collective-permute-start(f32[1,1,32,64]{3,2,1,0:T(8,128)S(1)} %get-tuple-element.273), channel_id=1, source_target_pairs={{0,1},{1,2},{2,3},{3,4},{4,5},{5,6},{6,7},{7,8},{8,9},{9,10},{10,1... | collective-permute-start | bytes 24584 | tf_op jit(solution)/shard_map/ppermute | solution.py:23
  346.0 9.0 %collective-permute-start.15 = (f32[1,1,32,64]{3,2,1,0:T(8,128)S(1)}, f32[1,1,32,64]{3,2,1,0:T(8,128)S(1)}, u32[]{:S(2)}, u32[]{:S(2)}) collective-permute-start(f32[1,1,32,64]{3,2,1,0:T(8,128)S(1)} %get-tuple-element.274), channel_id=1, source_target_pairs={{1,0},{2,1},{3,2},{4,3},{5,4},{6,5},{7,6},{8,7},{9,8},{10,9},{11,1... | collective-permute-start | bytes 24584 | tf_op jit(solution)/shard_map/ppermute | solution.py:24
  355.5 6.0 %collective-permute-start.16 = (f32[1,1,64,128]{3,2,1,0:T(8,128)S(1)}, f32[1,1,64,128]{3,2,1,0:T(8,128)S(1)}, u32[]{:S(2)}, u32[]{:S(2)}) collective-permute-start(f32[1,1,64,128]{3,2,1,0:T(8,128)S(1)} %get-tuple-element.243), channel_id=1, source_target_pairs={{0,1},{1,2},{2,3},{3,4},{4,5},{5,6},{6,7},{7,8},{8,9},{9,10},{10,1... | collective-permute-start | bytes 98312 | tf_op jit(solution)/shard_map/ppermute | solution.py:23
  357.5 9.1 %collective-permute-start.17 = (f32[1,1,64,128]{3,2,1,0:T(8,128)S(1)}, f32[1,1,64,128]{3,2,1,0:T(8,128)S(1)}, u32[]{:S(2)}, u32[]{:S(2)}) collective-permute-start(f32[1,1,64,128]{3,2,1,0:T(8,128)S(1)} %get-tuple-element.244), channel_id=1, source_target_pairs={{1,0},{2,1},{3,2},{4,3},{5,4},{6,5},{7,6},{8,7},{9,8},{10,9},{11,1... | collective-permute-start | bytes 98312 | tf_op jit(solution)/shard_map/ppermute | solution.py:24
  366.9 6.0 %collective-permute-start.18 = (f32[1,1,64,128]{3,2,1,0:T(8,128)S(1)}, f32[1,1,64,128]{3,2,1,0:T(8,128)S(1)}, u32[]{:S(2)}, u32[]{:S(2)}) collective-permute-start(f32[1,1,64,128]{3,2,1,0:T(8,128)S(1)} %get-tuple-element.237), channel_id=1, source_target_pairs={{0,1},{1,2},{2,3},{3,4},{4,5},{5,6},{6,7},{7,8},{8,9},{9,10},{10,1... | collective-permute-start | bytes 98312 | tf_op jit(solution)/shard_map/ppermute | solution.py:23
  368.8 9.1 %collective-permute-start.19 = (f32[1,1,64,128]{3,2,1,0:T(8,128)S(1)}, f32[1,1,64,128]{3,2,1,0:T(8,128)S(1)}, u32[]{:S(2)}, u32[]{:S(2)}) collective-permute-start(f32[1,1,64,128]{3,2,1,0:T(8,128)S(1)} %get-tuple-element.238), channel_id=1, source_target_pairs={{1,0},{2,1},{3,2},{4,3},{5,4},{6,5},{7,6},{8,7},{9,8},{10,9},{11,1... | collective-permute-start | bytes 98312 | tf_op jit(solution)/shard_map/ppermute | solution.py:24
  (24 other events, 1034.9 us)
Sparse Core Ops, SparseCore 0:
  9.2 27.4 all-gather.3
